TPU v7x, 32 devices: a whole 2x2x4 slice. The times are simulated.
32 devices in a mesh: dp: 8 (over y, x, core), shard: 4 (over z).
Axes of the slice: x: 2, y: 2, z: 4, core: 2. Of those that a mesh axis runs over, the one named last changes fastest.
Arguments:
- tokens: bfloat16 [8192, 1536], P(('dp', 'shard')), may hold values from -6 to 6
- cotangent: bfloat16 [8192, 1536], P(('dp', 'shard')), may hold values from -6 to 6
- seq_start: int32 [8192], P(('dp', 'shard')), may hold values from 0 to 192, as said below
- live_mask: int32 [8192], P(('dp', 'shard')), may hold values from 0 to 1, as said below
- input_proj: bfloat16 [2, 1536, 2048], P(None, None, 'shard'), may hold values from -0.15625 to 0.15625
- gate_blocks: bfloat16 [2, 16, 128, 128], P(None, 'shard'), may hold values from -0.5 to 0.5
- output_proj: bfloat16 [2048, 1536], P('shard'), may hold values from -0.375 to 0.375
- ffn_gate_up: bfloat16 [2, 1536, 4608], P(None, None, 'shard'), may hold values from -0.15625 to 0.15625
- ffn_down: bfloat16 [4608, 1536], P('shard'), may hold values from -0.1875 to 0.1875
- conv_taps: bfloat16 [5, 2048], P(None, 'shard'), may hold values from -3 to 3
- gate_bias: bfloat16 [2, 2048], P(None, 'shard'), may hold values from -3 to 3
- decay_param: bfloat16 [2048], P('shard'), may hold values from 3 to 8
- norm_gains: bfloat16 [2, 1536], P(None, 'shard'), may hold values from 0.5 to 1.5
- master_shard: float32 [4, 7803648], P('shard', 'dp'), may hold values from -0.75 to 0.75
- first_moment: float32 [4, 7803648], P('shard', 'dp'), may hold values from -6 to 6
- second_moment: float32 [4, 7803648], P('shard', 'dp'), may hold values from 0.1 to 10
Outputs:
- block_out: bfloat16 [8192, 1536], P(('dp', 'shard'))
- tokens_grad: bfloat16 [8192, 1536], P(('dp', 'shard'))
- weight_grads: float32 [4, 7803648], P('shard', 'dp')
- new_master: float32 [4, 7803648], P('shard', 'dp')
- new_first: float32 [4, 7803648], P('shard', 'dp')
- new_second: float32 [4, 7803648], P('shard', 'dp')
- new_weights: bfloat16 [4, 7803648], P(None, 'dp')
- bias_grad: float32 [2, 2048], P(None, 'shard')
Inputs may be any that keep to these rules, and one draw needn't show every extreme that they name: Within each device's block of 256 slots the live slots form a prefix of 2, 3 or 4 times 256 // 4 slots, and some device has all its slots live; every sequence begins at a multiple of 64, and every live sequence has 64 slots or more; seq_start is constant over a sequence and equals its first slot; the block holds one to four live sequences, and its padding forms one more sequence. `live_mask`: 1 exactly on the live prefix of each device's block.
All inputs are finite; a program needn't handle non-finite values.
Results may differ from a plain program's by a relative error of at most 0.017.
Values may be sent and summed in bfloat16 or wider, within the bound.
A program may use at most 384 MiB of HBM per device.

v0:
```python
import jax
import jax.numpy as jnp
from jax import lax
from jax.sharding import PartitionSpec as P

norm_eps = 1e-06
gate_scale = 8.0
beta_one = 0.9
beta_two = 0.95
learn_rate = 0.01
weight_decay = 0.1
adam_eps = 1e-08
corr_one = 1.0 - beta_one**10.0
corr_two = 1.0 - beta_two**10.0


def rms_scale(values, gain):
    return values * lax.rsqrt(jnp.mean(values * values, axis=-1, keepdims=True) + norm_eps) * gain


def conv_mix(signal, taps, position):
    result = taps[-1] + taps[0] * signal
    for shift_by in range(1, taps.shape[0] - 1):
        moved = jnp.pad(signal, ((shift_by, 0), (0, 0)))[:-shift_by]
        result = result + taps[shift_by] * jnp.where((position >= shift_by)[:, None], moved, 0.0)
    return result


def combine_steps(earlier, later):
    decay_first, value_first = earlier
    decay_second, value_second = later
    return (decay_first * decay_second, decay_second * value_first + value_second)


def recurrence(logits, signal, branch, bias_term, decay_term, position):
    row_count = signal.shape[0]
    recur_gate = jax.nn.sigmoid(logits[0].reshape(row_count, -1) + bias_term[0])
    input_gate = jax.nn.sigmoid(logits[1].reshape(row_count, -1) + bias_term[1])
    log_decay = -gate_scale * recur_gate * jax.nn.softplus(-decay_term)
    decay_rate = jnp.where((position > 0)[:, None], jnp.exp(log_decay), 0.0)
    drive_term = jnp.sqrt(-jnp.expm1(2.0 * log_decay)) * input_gate * signal
    states = lax.associative_scan(combine_steps, (decay_rate, drive_term), axis=0)[1]
    return states * jax.nn.gelu(branch)


def gated_gelu(ffn_pre):
    return jax.nn.gelu(ffn_pre[0]) * ffn_pre[1]


def mixer_forward(
    mix_in, input_proj, gate_blocks, output_proj, conv_taps, gate_bias, decay_param, position
):
    projected = jnp.einsum("sd,kdr->ksr", mix_in, input_proj, preferred_element_type=jnp.float32)
    conv_out, conv_pull = jax.vjp(
        lambda signal, taps: conv_mix(signal, taps, position), projected[0], conv_taps
    )
    row_count = conv_out.shape[0]
    conv_low = conv_out.astype(jnp.bfloat16).reshape(
        row_count, gate_blocks.shape[1], gate_blocks.shape[2]
    )
    gate_logits = jnp.einsum(
        "shb,khbc->kshc", conv_low, gate_blocks, preferred_element_type=jnp.float32
    )
    mixed, mix_pull = jax.vjp(
        lambda logits, signal, branch, bias_term, decay_term: recurrence(
            logits, signal, branch, bias_term, decay_term, position
        ),
        gate_logits,
        conv_out,
        projected[1],
        gate_bias,
        decay_param,
    )
    mixed_low = mixed.astype(jnp.bfloat16)
    partial_out = jnp.dot(mixed_low, output_proj, preferred_element_type=jnp.float32)
    return (partial_out, (conv_pull, conv_low, mix_pull, mixed_low))


def mixer_backward(grad_out_low, mix_in, saved, input_proj, gate_blocks, output_proj):
    conv_pull, conv_low, mix_pull, mixed_low = saved
    grad_output_proj = jnp.einsum(
        "sr,sd->rd", mixed_low, grad_out_low, preferred_element_type=jnp.float32
    )
    grad_mixed = jnp.einsum(
        "sd,rd->sr", grad_out_low, output_proj, preferred_element_type=jnp.float32
    )
    grad_logits, grad_conv_direct, grad_branch, grad_bias, grad_decay = mix_pull(grad_mixed)
    logits_low = grad_logits.astype(jnp.bfloat16)
    grad_blocks = jnp.einsum(
        "shb,kshc->khbc", conv_low, logits_low, preferred_element_type=jnp.float32
    )
    grad_conv_gates = jnp.einsum(
        "kshc,khbc->shb", logits_low, gate_blocks, preferred_element_type=jnp.float32
    )
    grad_signal, grad_taps = conv_pull(
        grad_conv_direct + grad_conv_gates.reshape(grad_conv_direct.shape)
    )
    proj_low = jnp.stack([grad_signal, grad_branch]).astype(jnp.bfloat16)
    grad_input_proj = jnp.einsum(
        "sd,ksr->kdr", mix_in, proj_low, preferred_element_type=jnp.float32
    )
    grad_mix_in = jnp.einsum(
        "ksr,kdr->sd", proj_low, input_proj, preferred_element_type=jnp.float32
    )
    return (
        grad_mix_in,
        (grad_input_proj, grad_blocks, grad_output_proj, grad_taps, grad_bias, grad_decay),
    )


def ffn_forward(ffn_in_low, ffn_gate_up, ffn_down):
    ffn_pre = jnp.einsum("sd,kdf->ksf", ffn_in_low, ffn_gate_up, preferred_element_type=jnp.float32)
    ffn_act, ffn_pull = jax.vjp(gated_gelu, ffn_pre)
    ffn_low = ffn_act.astype(jnp.bfloat16)
    partial_ffn = jnp.dot(ffn_low, ffn_down, preferred_element_type=jnp.float32)
    return (partial_ffn, (ffn_pull, ffn_low))


def ffn_backward(grad_low, ffn_in_low, saved, ffn_gate_up, ffn_down):
    ffn_pull, ffn_low = saved
    grad_down = jnp.einsum("sf,sd->fd", ffn_low, grad_low, preferred_element_type=jnp.float32)
    grad_act = jnp.einsum("sd,fd->sf", grad_low, ffn_down, preferred_element_type=jnp.float32)
    grad_pre = ffn_pull(grad_act)[0]
    pre_low = grad_pre.astype(jnp.bfloat16)
    grad_gate_up = jnp.einsum(
        "sd,ksf->kdf", ffn_in_low, pre_low, preferred_element_type=jnp.float32
    )
    grad_ffn_in = jnp.einsum(
        "ksf,kdf->sd", pre_low, ffn_gate_up, preferred_element_type=jnp.float32
    )
    return (grad_ffn_in, grad_gate_up, grad_down)


def body(
    tokens,
    cotangent,
    seq_start,
    live_mask,
    input_proj,
    gate_blocks,
    output_proj,
    ffn_gate_up,
    ffn_down,
    conv_taps,
    gate_bias,
    decay_param,
    norm_gains,
    master_shard,
    first_moment,
    second_moment,
):
    slot_count = tokens.shape[0]
    position = jnp.arange(slot_count, dtype=jnp.int32) - seq_start
    mask_rows = live_mask.astype(jnp.float32)[:, None]
    stream = tokens.astype(jnp.float32)
    grad_stream = cotangent.astype(jnp.float32) * mask_rows
    shards = (
        input_proj,
        gate_blocks,
        output_proj,
        ffn_gate_up,
        ffn_down,
        conv_taps,
        gate_bias,
        decay_param,
        norm_gains,
    )
    (
        full_in,
        full_blocks,
        full_out,
        full_up,
        full_down,
        full_taps,
        full_bias,
        full_decay,
        full_gains,
    ) = (
        lax.all_gather(shards[0], "shard", axis=2, tiled=True),
        lax.all_gather(shards[1], "shard", axis=1, tiled=True),
        lax.all_gather(shards[2], "shard", axis=0, tiled=True),
        lax.all_gather(shards[3], "shard", axis=2, tiled=True),
        lax.all_gather(shards[4], "shard", axis=0, tiled=True),
        lax.all_gather(shards[5], "shard", axis=1, tiled=True),
        lax.all_gather(shards[6], "shard", axis=1, tiled=True),
        lax.all_gather(shards[7], "shard", axis=0, tiled=True),
        lax.all_gather(shards[8], "shard", axis=1, tiled=True),
    )
    gains = full_gains.astype(jnp.float32)
    normed, norm_pull = jax.vjp(rms_scale, stream, gains[0])
    mix_in = normed.astype(jnp.bfloat16)
    mix_out, mix_saved = mixer_forward(
        mix_in,
        full_in,
        full_blocks,
        full_out,
        full_taps.astype(jnp.float32),
        full_bias.astype(jnp.float32),
        full_decay.astype(jnp.float32),
        position,
    )
    residual = stream + mix_out
    normed_two, second_pull = jax.vjp(rms_scale, residual, gains[1])
    ffn_in_low = normed_two.astype(jnp.bfloat16)
    ffn_result, ffn_saved = ffn_forward(ffn_in_low, full_up, full_down)
    block_out = (mask_rows * (residual + ffn_result)).astype(jnp.bfloat16)
    grad_ffn_in, grad_up, grad_down = ffn_backward(
        grad_stream.astype(jnp.bfloat16), ffn_in_low, ffn_saved, full_up, full_down
    )
    grad_norm_two, grad_gain_two = second_pull(grad_ffn_in)
    grad_residual = grad_stream + grad_norm_two
    grad_mix_in, mix_grads = mixer_backward(
        grad_residual.astype(jnp.bfloat16), mix_in, mix_saved, full_in, full_blocks, full_out
    )
    grad_norm_one, grad_gain_one = norm_pull(grad_mix_in)
    tokens_grad = (grad_residual + grad_norm_one).astype(jnp.bfloat16)
    grads = (
        mix_grads[0],
        mix_grads[1],
        mix_grads[2],
        grad_up,
        grad_down,
        mix_grads[3],
        mix_grads[4],
        mix_grads[5],
        jnp.stack([grad_gain_one, grad_gain_two]),
    )
    summed = (
        lax.psum_scatter(
            grads[0].astype(jnp.bfloat16), "shard", scatter_dimension=2, tiled=True
        ).astype(jnp.float32),
        lax.psum_scatter(
            grads[1].astype(jnp.bfloat16), "shard", scatter_dimension=1, tiled=True
        ).astype(jnp.float32),
        lax.psum_scatter(
            grads[2].astype(jnp.bfloat16), "shard", scatter_dimension=0, tiled=True
        ).astype(jnp.float32),
        lax.psum_scatter(
            grads[3].astype(jnp.bfloat16), "shard", scatter_dimension=2, tiled=True
        ).astype(jnp.float32),
        lax.psum_scatter(
            grads[4].astype(jnp.bfloat16), "shard", scatter_dimension=0, tiled=True
        ).astype(jnp.float32),
        lax.psum_scatter(
            grads[5].astype(jnp.bfloat16), "shard", scatter_dimension=1, tiled=True
        ).astype(jnp.float32),
        lax.psum_scatter(
            grads[6].astype(jnp.bfloat16), "shard", scatter_dimension=1, tiled=True
        ).astype(jnp.float32),
        lax.psum_scatter(
            grads[7].astype(jnp.bfloat16), "shard", scatter_dimension=0, tiled=True
        ).astype(jnp.float32),
        lax.psum_scatter(
            grads[8].astype(jnp.bfloat16), "shard", scatter_dimension=1, tiled=True
        ).astype(jnp.float32),
    )
    flat = jnp.concatenate([member.reshape(1, -1) for member in summed], axis=1)
    piece = lax.psum_scatter(flat, "dp", scatter_dimension=1, tiled=True)
    bias_total = lax.psum(summed[6], "dp")
    new_first = beta_one * first_moment + (1.0 - beta_one) * piece
    new_second = beta_two * second_moment + (1.0 - beta_two) * piece * piece
    new_master = master_shard - learn_rate * (
        new_first / corr_one / (jnp.sqrt(new_second / corr_two) + adam_eps)
        + weight_decay * master_shard
    )
    new_weights = lax.all_gather(new_master.astype(jnp.bfloat16), "shard", axis=0, tiled=True)
    return (
        block_out,
        tokens_grad,
        piece,
        new_master,
        new_first,
        new_second,
        new_weights,
        bias_total,
    )


def solution(mesh):
    placed = (
        P(("dp", "shard"), None),
        P(("dp", "shard"), None),
        P(("dp", "shard")),
        P(("dp", "shard")),
        P(None, None, "shard"),
        P(None, "shard", None, None),
        P("shard", None),
        P(None, None, "shard"),
        P("shard", None),
        P(None, "shard"),
        P(None, "shard"),
        P("shard"),
        P(None, "shard"),
        P("shard", "dp"),
        P("shard", "dp"),
        P("shard", "dp"),
    )
    return jax.shard_map(
        body,
        mesh=mesh,
        in_specs=placed,
        out_specs=(
            P(("dp", "shard"), None),
            P(("dp", "shard"), None),
            P("shard", "dp"),
            P("shard", "dp"),
            P("shard", "dp"),
            P("shard", "dp"),
            P(None, "dp"),
            P(None, "shard"),
        ),
        check_vma=False,
    )
```

profile of v0, /device:TPU:0, one launch (start us, length us, event | category | flops | bytes accessed | tf_op | source)
XLA Modules:
  0.0 3224.1 jit_solution(12165404766030103313)
XLA Ops:
  10.9 13.5 all_gather.31
  25.1 19.5 all-gather
  44.6 14.4 all_gather.34
  59.0 20.0 all_gather.30
  80.1 151.1 %all-gather.9.cloned.1.call-done = bf16[2,1536,2048]{2,1,0:T(8,128)(2,1)} async-done(((bf16[2,1536,512]{2,1,0:T(8,128)(2,1)}), bf16[2,1536,2048]{2,1,0:T(8,128)(2,1)}) %all-gather.9.cloned.1.call-update) | async-done | bytes 12582928 | tf_op jit(solution)/shard_map/all_gather | solution.py:179
  231.3 6.5 convolution_bitcast_fusion.1
  242.7 16.9 all-gather.11.cloned.1.call-done
  268.9 6.9 exponential_select_fusion
  365.9 5.6 slice.314
  400.4 8.5 pad.381
  412.2 8.5 pad.380
  426.3 6.2 multiply_reduce_fusion.7
  433.7 418.2 %all-gather.15.cloned.1.call-done = bf16[2,1536,4608]{2,1,0:T(8,128)(2,1)} async-done(((bf16[2,1536,1152]{2,1,0:T(8,128)(2,1)}), bf16[2,1536,4608]{2,1,0:T(8,128)(2,1)}) %all-gather.15.cloned.1.call-update) | async-done | bytes 28311568 | tf_op jit(solution)/shard_map/all_gather | solution.py:182
  851.9 19.1 convolution_bitcast_fusion
  870.9 224.5 %all-gather.17.cloned.1.call-done = bf16[4608,1536]{1,0:T(8,128)(2,1)} async-done(((bf16[1152,1536]{1,0:T(8,128)(2,1)}), bf16[4608,1536]{1,0:T(8,128)(2,1)}) %all-gather.17.cloned.1.call-update) | async-done | bytes 14155792 | tf_op jit(solution)/shard_map/all_gather | solution.py:183
  1095.4 14.4 multiply_bitcast_fusion
  1109.9 17.7 multiply_reduce_fusion.5
  1131.7 7.3 fusion.44
  1250.7 8.6 pad.435
  1264.1 8.6 pad.458
  1277.5 8.7 pad.436
  1286.2 8.8 pad.386
  1299.8 7.7 multiply_reduce_fusion
  1324.5 8.4 multiply_reduce_fusion.4
  1335.2 9.6 fusion.30
  1352.7 6.0 convolution_convert_fusion.1
  1360.2 6.5 convert_bitcast_fusion.1
  1367.9 9.3 convolution_convert_fusion
  1379.0 9.1 all-reduce.92
  1388.2 16.6 convert_bitcast_fusion
  1407.9 27.5 reduce-scatter.16.cloned.1.call-done
  1436.5 111.2 %reduce-scatter.18.cloned.1.call-done = bf16[512,1536]{1,0:T(8,128)(2,1)} async-done(((bf16[2048,1536]{1,0:T(8,128)(2,1)}), bf16[512,1536]{1,0:T(8,128)(2,1)}) %reduce-scatter.18.cloned.1.call-update) | async-done | bytes 1572880 | tf_op jit(solution)/shard_map/reduce_scatter | solution.py:235
  1554.4 208.2 %reduce-scatter.14.cloned.1.call-done = bf16[2,1536,512]{1,2,0:T(8,128)(2,1)} async-done(((bf16[2,1536,2048]{1,2,0:T(8,128)(2,1)}), bf16[2,1536,512]{1,2,0:T(8,128)(2,1)}) %reduce-scatter.14.cloned.1.call-update) | async-done | bytes 3145744 | tf_op jit(solution)/shard_map/reduce_scatter | solution.py:229
  1768.1 14.6 reshape.196
  1782.7 6.4 constant_dynamic-update-slice_fusion.8
  1792.6 210.6 %reduce-scatter.22.cloned.1.call-done = bf16[1152,1536]{1,0:T(8,128)(2,1)} async-done(((bf16[4608,1536]{1,0:T(8,128)(2,1)}), bf16[1152,1536]{1,0:T(8,128)(2,1)}) %reduce-scatter.22.cloned.1.call-update) | async-done | bytes 3538960 | tf_op jit(solution)/shard_map/reduce_scatter | solution.py:241
  2006.2 24.6 copy.106
  2030.8 440.8 %reduce-scatter.20.cloned.1.call-done = bf16[2,1536,1152]{1,2,0:T(8,128)(2,1)} async-done(((bf16[2,1536,4608]{1,2,0:T(8,128)(2,1)}), bf16[2,1536,1152]{1,2,0:T(8,128)(2,1)}) %reduce-scatter.20.cloned.1.call-update) | async-done | bytes 7077904 | tf_op jit(solution)/shard_map/reduce_scatter | solution.py:238
  2471.6 11.1 copy.80
  2482.6 27.7 reshape.202
  2510.4 10.3 constant_dynamic-update-slice_fusion.5
  2520.7 6.2 constant_dynamic-update-slice_fusion.4
  2531.2 374.5 %all-reduce.96.cloned.1.call-done = f32[1,7803648]{1,0:T(1,128)} async-done(((f32[1,7803648]{1,0:T(1,128)}), f32[1,7803648]{1,0:T(1,128)}) %all-reduce.96.cloned.1.call-update) | async-done | bytes 31214608
  2905.6 30.9 convert_bitcast_fusion.3
  2940.6 9.5 fusion.9
  2950.1 12.8 psum.7
  2962.8 241.6 %all-gather.19.cloned.1.call-done = bf16[4,1,975456]{2,1,0:T(2,128)(2,1)} async-done(((bf16[1,1,975456]{2,1,0:T(2,128)(2,1)}), bf16[4,1,975456]{2,1,0:T(2,128)(2,1)}) %all-gather.19.cloned.1.call-update) | async-done | bytes 7803664 | tf_op jit(solution)/shard_map/all_gather | solution.py:266
  3204.4 12.8 copy.115
  (553 shorter events, 338.5 us)
Async XLA Ops:
  7.2 224.1 %all-gather.9.cloned.1.call-start = ((), (), s32[]{:S(2)}) async-start(), calls=%async_computation.8 | async-start | bytes 15728640 | tf_op jit(solution)/shard_map/all_gather | solution.py:179
  7.9 251.7 %all-gather.11.cloned.1.call-start = ((), (), s32[]{:S(2)}) async-start(), calls=%async_computation.9 | async-start | bytes 1310720 | tf_op jit(solution)/shard_map/all_gather | solution.py:180
  8.9 417.5 %all-gather.13.cloned.1.call-start = ((), (), s32[]{:S(2)}) async-start(), calls=%async_computation.10 | async-start | bytes 7864320 | tf_op jit(solution)/shard_map/all_gather | solution.py:181
  9.6 842.3 %all-gather.15.cloned.1.call-start = ((), (), s32[]{:S(2)}) async-start(), calls=%async_computation.11 | async-start | bytes 35389440 | tf_op jit(solution)/shard_map/all_gather | solution.py:182
  10.2 14.3 copy-start.132
  10.2 14.3 copy-start.134
  10.2 34.4 %copy-start.130 = (bf16[2,512]{1,0:T(2,128)(2,1)S(1)}, bf16[2,512]{1,0:T(2,128)(2,1)}, u32[]{:S(2)}) copy-start(bf16[2,512]{1,0:T(2,128)(2,1)} %param.26) | copy-start | bytes 6148
  10.2 48.8 %copy-start.125 = (bf16[5,512]{1,0:T(8,128)(2,1)S(1)}, bf16[5,512]{1,0:T(8,128)(2,1)}, u32[]{:S(2)}) copy-start(bf16[5,512]{1,0:T(8,128)(2,1)} %param.25) | copy-start | bytes 15364
  10.2 68.8 %copy-start.11 = (bf16[256,1536]{1,0:T(8,128)(2,1)S(1)}, bf16[256,1536]{1,0:T(8,128)(2,1)}, u32[]{:S(2)}) copy-start(bf16[256,1536]{1,0:T(8,128)(2,1)} %param.16) | copy-start | bytes 2359300
  10.2 69.6 %copy-start.133 = (s32[256]{0:T(256)S(1)}, s32[256]{0:T(256)}, u32[]{:S(2)}) copy-start(s32[256]{0:T(256)} %param.18) | copy-start | bytes 3076
  10.3 1085.2 %all-gather.17.cloned.1.call-start = ((), (), s32[]{:S(2)}) async-start(), calls=%async_computation.12 | async-start | bytes 17694720 | tf_op jit(solution)/shard_map/all_gather | solution.py:183
  10.8 1394.0 %reduce-scatter.28.cloned.1.call-start = ((), (), s32[]{:S(2)}) async-start(), calls=%async_computation.21 | async-start | bytes 491520
  79.1 152.2 %copy-start.83 = (f32[1536]{0:T(1024)}, f32[1536]{0:T(1024)S(1)}, u32[]{:S(2)}) copy-start(f32[1536]{0:T(1024)S(1)} %get-tuple-element.18) | copy-start | bytes 18436
  79.9 151.4 %copy-start.114 = (f32[256]{0:T(256)}, f32[256]{0:T(256)S(1)}, u32[]{:S(2)}) copy-start(f32[256]{0:T(256)S(1)} %fusion.74) | copy-start | bytes 3076
  79.9 159.9 %copy-start.119 = (pred[256]{0:T(512)(128)(4,1)}, pred[256]{0:T(512)(128)(4,1)S(1)}, u32[]{:S(2)}) copy-start(pred[256]{0:T(512)(128)(4,1)S(1)} %get-tuple-element.142) | copy-start | bytes 772
  79.9 159.9 %copy-start.121 = (pred[256]{0:T(512)(128)(4,1)}, pred[256]{0:T(512)(128)(4,1)S(1)}, u32[]{:S(2)}) copy-start(pred[256]{0:T(512)(128)(4,1)S(1)} %get-tuple-element.143) | copy-start | bytes 772
  79.9 159.9 %copy-start.123 = (pred[256]{0:T(512)(128)(4,1)}, pred[256]{0:T(512)(128)(4,1)S(1)}, u32[]{:S(2)}) copy-start(pred[256]{0:T(512)(128)(4,1)S(1)} %get-tuple-element.144) | copy-start | bytes 772
  79.9 189.0 %copy-start.126 = (pred[256]{0:T(512)(128)(4,1)}, pred[256]{0:T(512)(128)(4,1)S(1)}, u32[]{:S(2)}) copy-start(pred[256]{0:T(512)(128)(4,1)S(1)} %get-tuple-element.141) | copy-start | bytes 772
  80.0 151.3 %copy-start.97 = (f32[4,1,512]{2,1,0:T(1,128)}, f32[4,1,512]{2,1,0:T(1,128)S(1)}, u32[]{:S(2)}) copy-start(f32[4,1,512]{2,1,0:T(1,128)S(1)} %convert_negate_fusion) | copy-start | bytes 24580
  80.0 188.9 %copy-start.85 = (f32[2048]{0:T(1024)}, f32[2048]{0:T(1024)S(1)}, u32[]{:S(2)}) copy-start(f32[2048]{0:T(1024)S(1)} %broadcast_multiply_fusion) | copy-start | bytes 24580
  80.0 188.9 %copy-start.87 = (f32[1,2048]{1,0:T(1,128)}, f32[1,2048]{1,0:T(1,128)S(1)}, u32[]{:S(2)}) copy-start(f32[1,2048]{1,0:T(1,128)S(1)} %get-tuple-element.139) | copy-start | bytes 24580
  80.0 188.9 %copy-start.89 = (f32[1,2048]{1,0:T(1,128)}, f32[1,2048]{1,0:T(1,128)S(1)}, u32[]{:S(2)}) copy-start(f32[1,2048]{1,0:T(1,128)S(1)} %get-tuple-element.140) | copy-start | bytes 24580
  80.1 159.7 %copy-start.99 = (f32[1,2048]{1,0:T(1,128)}, f32[1,2048]{1,0:T(1,128)S(1)}, u32[]{:S(2)}) copy-start(f32[1,2048]{1,0:T(1,128)S(1)} %get-tuple-element.123) | copy-start | bytes 24580
  80.1 159.7 %copy-start.101 = (f32[1,2048]{1,0:T(1,128)}, f32[1,2048]{1,0:T(1,128)S(1)}, u32[]{:S(2)}) copy-start(f32[1,2048]{1,0:T(1,128)S(1)} %get-tuple-element.124) | copy-start | bytes 24580
  80.1 159.7 %copy-start.103 = (f32[1,2048]{1,0:T(1,128)}, f32[1,2048]{1,0:T(1,128)S(1)}, u32[]{:S(2)}) copy-start(f32[1,2048]{1,0:T(1,128)S(1)} %get-tuple-element.125) | copy-start | bytes 24580
  80.1 159.7 %copy-start.105 = (f32[1,2048]{1,0:T(1,128)}, f32[1,2048]{1,0:T(1,128)S(1)}, u32[]{:S(2)}) copy-start(f32[1,2048]{1,0:T(1,128)S(1)} %get-tuple-element.126) | copy-start | bytes 24580
  242.7 18.9 copy-start.14
  321.3 37.7 %copy-start.51 = (f32[16,2048]{1,0:T(8,128)}, f32[16,2048]{1,0:T(8,128)S(1)}, u32[]{:S(2)}) copy-start(f32[16,2048]{1,0:T(8,128)S(1)} %slice.337) | copy-start | bytes 393220
  327.6 36.1 %copy-start.21 = (f32[128,2048]{1,0:T(8,128)S(1)}, f32[128,2048]{1,0:T(8,128)}, u32[]{:S(2)}) copy-start(f32[128,2048]{1,0:T(8,128)} %get-tuple-element.76) | copy-start | bytes 3145732
  365.9 13.4 copy-start.91
  365.9 14.4 copy-start.75
  365.9 14.4 copy-start.94
  365.9 14.4 copy-start.113
  1178.9 15.4 copy-start.72
  1181.6 14.1 copy-start.71
  1183.8 13.5 copy-start.32
  1183.8 13.5 slice-start.3
  1233.2 14.0 copy-start.8
  1233.2 14.0 slice-start.1
  1345.9 60.0 %reduce-scatter.26.cloned.1.call-start = ((), (), s32[]{:S(2)}) async-start(), calls=%async_computation.20 | async-start | bytes 655360
  1347.0 60.1 %reduce-scatter.24.cloned.1.call-start = ((), (), s32[]{:S(2)}) async-start(), calls=%async_computation.18 | async-start | bytes 40960 | tf_op jit(solution)/shard_map/reduce_scatter | solution.py:244
  1347.8 87.6 %reduce-scatter.16.cloned.1.call-start = ((), (), s32[]{:S(2)}) async-start(), calls=%async_computation.14 | async-start | bytes 1310720 | tf_op jit(solution)/shard_map/reduce_scatter | solution.py:232
  1351.5 196.2 %reduce-scatter.18.cloned.1.call-start = ((), (), s32[]{:S(2)}) async-start(), calls=%async_computation.15 | async-start | bytes 7864320 | tf_op jit(solution)/shard_map/reduce_scatter | solution.py:235
  1358.7 403.9 %reduce-scatter.14.cloned.1.call-start = ((), (), s32[]{:S(2)}) async-start(), calls=%async_computation.13 | async-start | bytes 15728640 | tf_op jit(solution)/shard_map/reduce_scatter | solution.py:229
  1366.8 636.5 %reduce-scatter.22.cloned.1.call-start = ((), (), s32[]{:S(2)}) async-start(), calls=%async_computation.17 | async-start | bytes 17694720 | tf_op jit(solution)/shard_map/reduce_scatter | solution.py:241
  1377.2 1094.4 %reduce-scatter.20.cloned.1.call-start = ((), (), s32[]{:S(2)}) async-start(), calls=%async_computation.16 | async-start | bytes 35389440 | tf_op jit(solution)/shard_map/reduce_scatter | solution.py:238
  1404.8 1500.9 %all-reduce.96.cloned.1.call-start = ((), (), s32[]{:S(2)}) async-start(), calls=%async_computation.22 | async-start | bytes 62429184
  2529.3 675.1 %all-gather.19.cloned.1.call-start = ((), (), s32[]{:S(2)}) async-start(), calls=%async_computation.19 | async-start | bytes 19509760 | tf_op jit(solution)/shard_map/all_gather | solution.py:266
  (108 other events, 576.2 us)
Sparse Core Ops, SparseCore 0:
  9.6 221.6 all-gather.8
  233.4 26.1 all-gather.10
  261.2 114.8 all-gather.12
  377.5 474.3 all-gather.14
  853.3 242.1 all-gather.16
  1346.0 18.7 reduce-scatter.27
  1367.8 19.9 reduce-scatter.25
  1390.0 17.0 reduce-scatter.23
  1410.1 25.3 reduce-scatter.15
  1438.2 109.4 reduce-scatter.17
  1550.2 212.3 reduce-scatter.13
  1764.9 238.2 reduce-scatter.21
  2005.7 465.8 reduce-scatter.19
  2529.4 376.1 all-reduce.95
  2936.7 267.6 all-gather.18
where the time goes:
time: 3240 us; the launch traced here: 3220 us
  waiting for transfers between devices  2430 us (75%)
  local copies, waits for them, and re-layouts  407 us (13%)
  other arithmetic  144 us (4%)
  matrix products  138 us (4%)
  blocking collectives  89.4 us (3%)
    reduce_scatter x1, waiting for transfers between devices, body(): lax.psum_scatter(grads[3].astype(jnp.bfloat16), 'shard', scatter_dimensio...  441 us
    all_gather x1, waiting for transfers between devices, body(): lax.all_gather(shards[3], 'shard', axis=2, tiled=True)  418 us
    unnamed x18, waiting for transfers between devices  377 us
    all_gather x1, waiting for transfers between devices, body(): lax.all_gather(new_master.astype(jnp.bfloat16), 'shard', axis=0, tiled=True)  242 us
    all_gather x1, waiting for transfers between devices, body(): lax.all_gather(shards[4], 'shard', axis=0, tiled=True)  225 us
    reduce_scatter x1, waiting for transfers between devices, body(): lax.psum_scatter(grads[4].astype(jnp.bfloat16), 'shard', scatter_dimensio...  211 us
    reduce_scatter x1, waiting for transfers between devices, body(): lax.psum_scatter(grads[0].astype(jnp.bfloat16), 'shard', scatter_dimensio...  208 us
    all_gather x1, waiting for transfers between devices, body(): lax.all_gather(shards[0], 'shard', axis=2, tiled=True)  151 us
  transfers between devices with their start and end apart: 15, of which 12 were waited for; matrix products, arithmetic and copies ran while one was open for 10% of the time, Pallas kernels for 0%

commit v1 on v0

--- a/solution.py
+++ b/solution.py
@@ -263,7 +263,24 @@
         new_first / corr_one / (jnp.sqrt(new_second / corr_two) + adam_eps)
         + weight_decay * master_shard
     )
-    new_weights = lax.all_gather(new_master.astype(jnp.bfloat16), "shard", axis=0, tiled=True)
+    x = new_master.astype(jnp.bfloat16)
+    length, index, rows = (lax.axis_size("shard"), lax.axis_index("shard"), x.shape[0])
+    forward = [(i, (i + 1) % length) for i in range(length)]
+    behind = [(i, (i - 1) % length) for i in range(length)]
+    new_weights = jnp.zeros((*x.shape[:0], length * rows, *x.shape[0 + 1 :]), x.dtype)
+    new_weights = lax.dynamic_update_slice_in_dim(new_weights, x, index * rows, axis=0)
+    from_left = from_right = x
+    halfway = length // 2
+    for step in range(1, halfway + 1):
+        from_left = lax.ppermute(from_left, "shard", forward)
+        new_weights = lax.dynamic_update_slice_in_dim(
+            new_weights, from_left, (index - step) % length * rows, axis=0
+        )
+        if step < length - halfway:
+            from_right = lax.ppermute(from_right, "shard", behind)
+            new_weights = lax.dynamic_update_slice_in_dim(
+                new_weights, from_right, (index + step) % length * rows, axis=0
+            )
     return (
         block_out,
         tokens_grad,

time: 3240 us -> 3360 us (1.037)
  local copies, waits for them, and re-layouts: 407 us -> 661 us
  waiting for transfers between devices: 2430 us -> 2270 us
    dynamic_update_slice x0 -> x4, local copies, waits for them, and re-layouts: none -> 265 us  [the longest x2 132 us: body(): lax.dynamic_update_slice_in_dim(new_weights, from_left, (index - step) %...]
    all_gather x1 -> x0, waiting for transfers between devices: 242 us -> none  [body(): lax.all_gather(new_master.astype(jnp.bfloat16), 'shard', axis=0, tiled=True)]
    ppermute x0 -> x3, waiting for transfers between devices: none -> 85.5 us  [the longest x2 85.5 us: body(): from_left = lax.ppermute(from_left, 'shard', forward)]
    unnamed x297 -> x308, local copies, waits for them, and re-layouts: 88.3 us -> 71.7 us
    unnamed x18 -> x17, waiting for transfers between devices: 377 us -> 377 us
  transfers between devices with their start and end apart: 15 -> 17, of which waited for: 12 -> 12; matrix products, arithmetic and copies ran while one was open for 10% -> 16% of each run, Pallas kernels for 0% -> 0%
where the time goes in v1:
time: 3360 us; the launch traced here: 3320 us
  waiting for transfers between devices  2270 us (68%)
  local copies, waits for them, and re-layouts  661 us (20%)
  other arithmetic  143 us (4%)
  matrix products  135 us (4%)
  blocking collectives  89 us (3%)
    reduce_scatter x1, waiting for transfers between devices, body(): lax.psum_scatter(grads[3].astype(jnp.bfloat16), 'shard', scatter_dimensio...  441 us
    all_gather x1, waiting for transfers between devices, body(): lax.all_gather(shards[3], 'shard', axis=2, tiled=True)  418 us
    unnamed x17, waiting for transfers between devices  377 us
    all_gather x1, waiting for transfers between devices, body(): lax.all_gather(shards[4], 'shard', axis=0, tiled=True)  225 us
    reduce_scatter x1, waiting for transfers between devices, body(): lax.psum_scatter(grads[4].astype(jnp.bfloat16), 'shard', scatter_dimensio...  211 us
    reduce_scatter x1, waiting for transfers between devices, body(): lax.psum_scatter(grads[0].astype(jnp.bfloat16), 'shard', scatter_dimensio...  210 us
    all_gather x1, waiting for transfers between devices, body(): lax.all_gather(shards[0], 'shard', axis=2, tiled=True)  151 us
    dynamic_update_slice x2, local copies, waits for them, and re-layouts, body(): lax.dynamic_update_slice_in_dim(new_weights, from_left, (index - step) %...  132 us
  transfers between devices with their start and end apart: 17, of which 12 were waited for; matrix products, arithmetic and copies ran while one was open for 16% of the time, Pallas kernels for 0%

profile of v1, /device:TPU:0, one launch (start us, length us, event | category | flops | bytes accessed | tf_op | source)
XLA Modules:
  0.0 3324.2 jit_solution(7266421348605102012)
XLA Ops:
  10.9 13.5 all_gather.28
  25.1 19.5 all-gather
  44.6 14.4 all_gather.31
  59.0 20.0 all_gather.27
  80.1 151.2 %all-gather.7.cloned.1.call-done = bf16[2,1536,2048]{2,1,0:T(8,128)(2,1)} async-done(((bf16[2,1536,512]{2,1,0:T(8,128)(2,1)}), bf16[2,1536,2048]{2,1,0:T(8,128)(2,1)}) %all-gather.7.cloned.1.call-update) | async-done | bytes 12582928 | tf_op jit(solution)/shard_map/all_gather | solution.py:179
  231.3 6.5 convolution_bitcast_fusion.1
  242.8 16.8 all-gather.9.cloned.1.call-done
  268.9 6.9 exponential_select_fusion
  400.4 8.6 pad.381
  412.2 8.5 pad.380
  426.3 6.2 multiply_reduce_fusion.7
  433.6 418.2 %all-gather.13.cloned.1.call-done = bf16[2,1536,4608]{2,1,0:T(8,128)(2,1)} async-done(((bf16[2,1536,1152]{2,1,0:T(8,128)(2,1)}), bf16[2,1536,4608]{2,1,0:T(8,128)(2,1)}) %all-gather.13.cloned.1.call-update) | async-done | bytes 28311568 | tf_op jit(solution)/shard_map/all_gather | solution.py:182
  851.9 18.9 convolution_bitcast_fusion
  870.8 224.6 %all-gather.15.cloned.1.call-done = bf16[4608,1536]{1,0:T(8,128)(2,1)} async-done(((bf16[1152,1536]{1,0:T(8,128)(2,1)}), bf16[4608,1536]{1,0:T(8,128)(2,1)}) %all-gather.15.cloned.1.call-update) | async-done | bytes 14155792 | tf_op jit(solution)/shard_map/all_gather | solution.py:183
  1095.4 14.4 multiply_bitcast_fusion
  1109.8 17.8 multiply_reduce_fusion.5
  1131.7 7.3 fusion.44
  1251.0 8.6 pad.435
  1264.5 8.6 pad.458
  1277.8 8.6 pad.436
  1286.4 8.8 pad.386
  1300.1 7.7 multiply_reduce_fusion
  1324.8 8.3 multiply_reduce_fusion.4
  1335.3 9.6 fusion.30
  1360.2 6.5 convert_bitcast_fusion.1
  1368.6 7.8 convolution_convert_fusion
  1378.2 9.2 all-reduce.92
  1387.4 16.6 convert_bitcast_fusion
  1408.0 27.5 reduce-scatter.16.cloned.1.call-done
  1437.4 110.4 %reduce-scatter.18.cloned.1.call-done = bf16[512,1536]{1,0:T(8,128)(2,1)} async-done(((bf16[2048,1536]{1,0:T(8,128)(2,1)}), bf16[512,1536]{1,0:T(8,128)(2,1)}) %reduce-scatter.18.cloned.1.call-update) | async-done | bytes 1572880 | tf_op jit(solution)/shard_map/reduce_scatter | solution.py:235
  1552.9 209.9 %reduce-scatter.14.cloned.1.call-done = bf16[2,1536,512]{1,2,0:T(8,128)(2,1)} async-done(((bf16[2,1536,2048]{1,2,0:T(8,128)(2,1)}), bf16[2,1536,512]{1,2,0:T(8,128)(2,1)}) %reduce-scatter.14.cloned.1.call-update) | async-done | bytes 3145744 | tf_op jit(solution)/shard_map/reduce_scatter | solution.py:229
  1768.2 14.6 reshape.196
  1782.8 6.2 constant_dynamic-update-slice_fusion.8
  1792.6 210.7 %reduce-scatter.22.cloned.1.call-done = bf16[1152,1536]{1,0:T(8,128)(2,1)} async-done(((bf16[4608,1536]{1,0:T(8,128)(2,1)}), bf16[1152,1536]{1,0:T(8,128)(2,1)}) %reduce-scatter.22.cloned.1.call-update) | async-done | bytes 3538960 | tf_op jit(solution)/shard_map/reduce_scatter | solution.py:241
  2006.3 24.6 copy.90
  2030.9 440.8 %reduce-scatter.20.cloned.1.call-done = bf16[2,1536,1152]{1,2,0:T(8,128)(2,1)} async-done(((bf16[2,1536,4608]{1,2,0:T(8,128)(2,1)}), bf16[2,1536,1152]{1,2,0:T(8,128)(2,1)}) %reduce-scatter.20.cloned.1.call-update) | async-done | bytes 7077904 | tf_op jit(solution)/shard_map/reduce_scatter | solution.py:238
  2471.7 11.0 copy.65
  2482.7 27.7 reshape.202
  2510.4 10.4 constant_dynamic-update-slice_fusion.5
  2529.0 374.5 %all-reduce.96.cloned.1.call-done = f32[1,7803648]{1,0:T(1,128)} async-done(((f32[1,7803648]{1,0:T(1,128)}), f32[1,7803648]{1,0:T(1,128)}) %all-reduce.96.cloned.1.call-update) | async-done | bytes 31214608
  2903.5 30.9 fusion.88
  2938.2 85.5 %collective-permute-done = bf16[1,975456]{1,0:T(2,128)(2,1)} collective-permute-done((bf16[1,975456]{1,0:T(2,128)(2,1)}, bf16[1,975456]{1,0:T(2,128)(2,1)}, u32[]{:S(2)}, u32[]{:S(2)}) %collective-permute-start) | collective-permute-done | bytes 1950944 | tf_op jit(solution)/shard_map/ppermute | solution.py:275
  3026.7 8.2 fusion.9
  3034.9 12.4 psum.7
  3052.3 66.2 %dynamic_update_slice.12 = bf16[4,975456]{1,0:T(4,128)(2,1)} dynamic-update-slice(bf16[4,975456]{1,0:T(4,128)(2,1)} %broadcast_in_dim.74, bf16[1,975456]{1,0:T(2,128)(2,1)} %get-tuple-element.19, s32[]{:T(128)S(6)} %select_n.76, s32[]{:T(128)} %constant.89.clone.1) | dynamic-update-slice | bytes 3901828 | tf_op jit(solution)/shard_map/dynamic_update_slice | solution.py:271
  3118.5 66.2 %dynamic_update_slice.13 = bf16[4,975456]{1,0:T(4,128)(2,1)} dynamic-update-slice(bf16[4,975456]{1,0:T(4,128)(2,1)} %dynamic_update_slice.12, bf16[1,975456]{1,0:T(2,128)(2,1)} %collective-permute-done, s32[]{:T(128)S(6)} %select_n.78, s32[]{:T(128)} %constant.89.clone.1) | dynamic-update-slice | bytes 3901828 | tf_op jit(solution)/shard_map/dynamic_update_slice | solution.py:276
  3184.8 66.2 %dynamic_update_slice.14 = bf16[4,975456]{1,0:T(4,128)(2,1)} dynamic-update-slice(bf16[4,975456]{1,0:T(4,128)(2,1)} %dynamic_update_slice.13, bf16[1,975456]{1,0:T(2,128)(2,1)} %collective-permute-done.1, s32[]{:T(128)S(6)} %select_n.80, s32[]{:T(128)} %constant.89.clone.1) | dynamic-update-slice | bytes 3901828 | tf_op jit(solution)/shard_map/dynamic_update_slice | solution.py:281
  3251.0 66.2 %dynamic_update_slice.15 = bf16[4,975456]{1,0:T(4,128)(2,1)} dynamic-update-slice(bf16[4,975456]{1,0:T(4,128)(2,1)} %dynamic_update_slice.14, bf16[1,975456]{1,0:T(2,128)(2,1)} %collective-permute-done.2, s32[]{:T(128)S(6)} %select_n.82, s32[]{:T(128)} %constant.89.clone.1) | dynamic-update-slice | bytes 3901828 | tf_op jit(solution)/shard_map/dynamic_update_slice | solution.py:276
  (573 shorter events, 362.6 us)
Async XLA Ops:
  7.2 224.1 %all-gather.7.cloned.1.call-start = ((), (), s32[]{:S(2)}) async-start(), calls=%async_computation.8 | async-start | bytes 15728640 | tf_op jit(solution)/shard_map/all_gather | solution.py:179
  7.9 251.7 %all-gather.9.cloned.1.call-start = ((), (), s32[]{:S(2)}) async-start(), calls=%async_computation.9 | async-start | bytes 1310720 | tf_op jit(solution)/shard_map/all_gather | solution.py:180
  8.9 417.5 %all-gather.11.cloned.1.call-start = ((), (), s32[]{:S(2)}) async-start(), calls=%async_computation.10 | async-start | bytes 7864320 | tf_op jit(solution)/shard_map/all_gather | solution.py:181
  9.6 842.3 %all-gather.13.cloned.1.call-start = ((), (), s32[]{:S(2)}) async-start(), calls=%async_computation.11 | async-start | bytes 35389440 | tf_op jit(solution)/shard_map/all_gather | solution.py:182
  10.2 14.3 copy-start.136
  10.2 14.3 copy-start.138
  10.2 34.4 %copy-start.134 = (bf16[2,512]{1,0:T(2,128)(2,1)S(1)}, bf16[2,512]{1,0:T(2,128)(2,1)}, u32[]{:S(2)}) copy-start(bf16[2,512]{1,0:T(2,128)(2,1)} %param.26) | copy-start | bytes 6148
  10.2 48.8 %copy-start.129 = (bf16[5,512]{1,0:T(8,128)(2,1)S(1)}, bf16[5,512]{1,0:T(8,128)(2,1)}, u32[]{:S(2)}) copy-start(bf16[5,512]{1,0:T(8,128)(2,1)} %param.25) | copy-start | bytes 15364
  10.2 68.8 %copy-start.13 = (bf16[256,1536]{1,0:T(8,128)(2,1)S(1)}, bf16[256,1536]{1,0:T(8,128)(2,1)}, u32[]{:S(2)}) copy-start(bf16[256,1536]{1,0:T(8,128)(2,1)} %param.16) | copy-start | bytes 2359300
  10.2 69.6 %copy-start.137 = (s32[256]{0:T(256)S(1)}, s32[256]{0:T(256)}, u32[]{:S(2)}) copy-start(s32[256]{0:T(256)} %param.18) | copy-start | bytes 3076
  10.3 1085.2 %all-gather.15.cloned.1.call-start = ((), (), s32[]{:S(2)}) async-start(), calls=%async_computation.12 | async-start | bytes 17694720 | tf_op jit(solution)/shard_map/all_gather | solution.py:183
  10.8 1393.4 %reduce-scatter.28.cloned.1.call-start = ((), (), s32[]{:S(2)}) async-start(), calls=%async_computation.20 | async-start | bytes 491520
  79.1 158.7 %copy-start.87 = (f32[1536]{0:T(1024)}, f32[1536]{0:T(1024)S(1)}, u32[]{:S(2)}) copy-start(f32[1536]{0:T(1024)S(1)} %get-tuple-element.18) | copy-start | bytes 18436
  79.9 157.9 %copy-start.118 = (f32[256]{0:T(256)}, f32[256]{0:T(256)S(1)}, u32[]{:S(2)}) copy-start(f32[256]{0:T(256)S(1)} %fusion.74) | copy-start | bytes 3076
  79.9 159.9 %copy-start.123 = (pred[256]{0:T(512)(128)(4,1)}, pred[256]{0:T(512)(128)(4,1)S(1)}, u32[]{:S(2)}) copy-start(pred[256]{0:T(512)(128)(4,1)S(1)} %get-tuple-element.142) | copy-start | bytes 772
  79.9 159.9 %copy-start.125 = (pred[256]{0:T(512)(128)(4,1)}, pred[256]{0:T(512)(128)(4,1)S(1)}, u32[]{:S(2)}) copy-start(pred[256]{0:T(512)(128)(4,1)S(1)} %get-tuple-element.143) | copy-start | bytes 772
  79.9 159.9 %copy-start.127 = (pred[256]{0:T(512)(128)(4,1)}, pred[256]{0:T(512)(128)(4,1)S(1)}, u32[]{:S(2)}) copy-start(pred[256]{0:T(512)(128)(4,1)S(1)} %get-tuple-element.144) | copy-start | bytes 772
  79.9 189.0 %copy-start.130 = (pred[256]{0:T(512)(128)(4,1)}, pred[256]{0:T(512)(128)(4,1)S(1)}, u32[]{:S(2)}) copy-start(pred[256]{0:T(512)(128)(4,1)S(1)} %get-tuple-element.141) | copy-start | bytes 772
  79.9 157.9 %copy-start.101 = (f32[4,1,512]{2,1,0:T(1,128)}, f32[4,1,512]{2,1,0:T(1,128)S(1)}, u32[]{:S(2)}) copy-start(f32[4,1,512]{2,1,0:T(1,128)S(1)} %convert_negate_fusion) | copy-start | bytes 24580
  80.0 188.9 %copy-start.89 = (f32[2048]{0:T(1024)}, f32[2048]{0:T(1024)S(1)}, u32[]{:S(2)}) copy-start(f32[2048]{0:T(1024)S(1)} %broadcast_multiply_fusion) | copy-start | bytes 24580
  80.0 188.9 %copy-start.91 = (f32[1,2048]{1,0:T(1,128)}, f32[1,2048]{1,0:T(1,128)S(1)}, u32[]{:S(2)}) copy-start(f32[1,2048]{1,0:T(1,128)S(1)} %get-tuple-element.139) | copy-start | bytes 24580
  80.0 188.9 %copy-start.93 = (f32[1,2048]{1,0:T(1,128)}, f32[1,2048]{1,0:T(1,128)S(1)}, u32[]{:S(2)}) copy-start(f32[1,2048]{1,0:T(1,128)S(1)} %get-tuple-element.140) | copy-start | bytes 24580
  80.0 159.8 %copy-start.103 = (f32[1,2048]{1,0:T(1,128)}, f32[1,2048]{1,0:T(1,128)S(1)}, u32[]{:S(2)}) copy-start(f32[1,2048]{1,0:T(1,128)S(1)} %get-tuple-element.123) | copy-start | bytes 24580
  80.1 159.8 %copy-start.105 = (f32[1,2048]{1,0:T(1,128)}, f32[1,2048]{1,0:T(1,128)S(1)}, u32[]{:S(2)}) copy-start(f32[1,2048]{1,0:T(1,128)S(1)} %get-tuple-element.124) | copy-start | bytes 24580
  80.1 159.8 %copy-start.107 = (f32[1,2048]{1,0:T(1,128)}, f32[1,2048]{1,0:T(1,128)S(1)}, u32[]{:S(2)}) copy-start(f32[1,2048]{1,0:T(1,128)S(1)} %get-tuple-element.125) | copy-start | bytes 24580
  80.1 159.8 %copy-start.109 = (f32[1,2048]{1,0:T(1,128)}, f32[1,2048]{1,0:T(1,128)S(1)}, u32[]{:S(2)}) copy-start(f32[1,2048]{1,0:T(1,128)S(1)} %get-tuple-element.126) | copy-start | bytes 24580
  242.7 18.8 copy-start.16
  321.3 37.8 %copy-start.55 = (f32[16,2048]{1,0:T(8,128)}, f32[16,2048]{1,0:T(8,128)S(1)}, u32[]{:S(2)}) copy-start(f32[16,2048]{1,0:T(8,128)S(1)} %slice.337) | copy-start | bytes 393220
  327.7 36.1 %copy-start.23 = (f32[128,2048]{1,0:T(8,128)S(1)}, f32[128,2048]{1,0:T(8,128)}, u32[]{:S(2)}) copy-start(f32[128,2048]{1,0:T(8,128)} %get-tuple-element.76) | copy-start | bytes 3145732
  366.0 14.3 copy-start.79
  366.0 14.3 copy-start.98
  366.0 14.4 copy-start.117
  1179.0 15.4 copy-start.76
  1345.9 59.3 %reduce-scatter.26.cloned.1.call-start = ((), (), s32[]{:S(2)}) async-start(), calls=%async_computation.19 | async-start | bytes 655360
  1347.1 60.2 %reduce-scatter.24.cloned.1.call-start = ((), (), s32[]{:S(2)}) async-start(), calls=%async_computation.18 | async-start | bytes 40960 | tf_op jit(solution)/shard_map/reduce_scatter | solution.py:244
  1347.8 87.7 %reduce-scatter.16.cloned.1.call-start = ((), (), s32[]{:S(2)}) async-start(), calls=%async_computation.14 | async-start | bytes 1310720 | tf_op jit(solution)/shard_map/reduce_scatter | solution.py:232
  1351.5 196.3 %reduce-scatter.18.cloned.1.call-start = ((), (), s32[]{:S(2)}) async-start(), calls=%async_computation.15 | async-start | bytes 7864320 | tf_op jit(solution)/shard_map/reduce_scatter | solution.py:235
  1358.7 404.0 %reduce-scatter.14.cloned.1.call-start = ((), (), s32[]{:S(2)}) async-start(), calls=%async_computation.13 | async-start | bytes 15728640 | tf_op jit(solution)/shard_map/reduce_scatter | solution.py:229
  1366.8 636.6 %reduce-scatter.22.cloned.1.call-start = ((), (), s32[]{:S(2)}) async-start(), calls=%async_computation.17 | async-start | bytes 17694720 | tf_op jit(solution)/shard_map/reduce_scatter | solution.py:241
  1376.4 1095.3 %reduce-scatter.20.cloned.1.call-start = ((), (), s32[]{:S(2)}) async-start(), calls=%async_computation.16 | async-start | bytes 35389440 | tf_op jit(solution)/shard_map/reduce_scatter | solution.py:238
  1404.1 1499.4 %all-reduce.96.cloned.1.call-start = ((), (), s32[]{:S(2)}) async-start(), calls=%async_computation.21 | async-start | bytes 62429184
  2482.7 38.1 %slice-start = ((s8[7077888]{0:T(1024)(128)(4,1)}), s8[2883584]{0:T(1024)(128)(4,1)S(1)}, s32[]{:S(2)}) async-start(s8[7077888]{0:T(1024)(128)(4,1)} %bitcast.151), calls=%async_computation.22 | async-start | bytes 5767168
  2529.0 494.8 %copy-start.121 = (f32[256]{0:T(256)S(1)}, f32[256]{0:T(256)}, u32[]{:S(2)}) copy-start(f32[256]{0:T(256)} %copy-done.120) | copy-start | bytes 3076
  2529.0 494.8 %copy-start.12 = (f32[256,1536]{1,0:T(8,128)S(1)}, f32[256,1536]{1,0:T(8,128)}, u32[]{:S(2)}) copy-start(f32[256,1536]{1,0:T(8,128)} %copy-done.11) | copy-start | bytes 4718596
  2529.0 494.8 %copy-start.15 = (bf16[256,1536]{1,0:T(8,128)(2,1)S(1)}, bf16[256,1536]{1,0:T(8,128)(2,1)}, u32[]{:S(2)}) copy-start(bf16[256,1536]{1,0:T(8,128)(2,1)} %param.16) | copy-start | bytes 2359300
  2934.4 89.3 %collective-permute-start = (bf16[1,975456]{1,0:T(2,128)(2,1)}, bf16[1,975456]{1,0:T(2,128)(2,1)}, u32[]{:S(2)}, u32[]{:S(2)}) collective-permute-start(bf16[1,975456]{1,0:T(2,128)(2,1)} %get-tuple-element.19), channel_id=1, source_target_pairs={{0,1},{1,2},{2,3},{3,0},{4,5},{5,6},{6,7},{7,4},{8,9},{9,10},{10,1... | collective-permute-start | bytes 5852744 | tf_op jit(solution)/shard_map/ppermute | solution.py:275
  2935.9 248.8 %collective-permute-start.1 = (bf16[1,975456]{1,0:T(2,128)(2,1)}, bf16[1,975456]{1,0:T(2,128)(2,1)}, u32[]{:S(2)}, u32[]{:S(2)}) collective-permute-start(bf16[1,975456]{1,0:T(2,128)(2,1)} %get-tuple-element.19), channel_id=1, source_target_pairs={{0,3},{1,0},{2,1},{3,2},{4,7},{5,4},{6,5},{7,6},{8,11},{9,8},{10,9... | collective-permute-start | bytes 5852744 | tf_op jit(solution)/shard_map/ppermute | solution.py:280
  3023.7 227.2 %collective-permute-start.2 = (bf16[1,975456]{1,0:T(2,128)(2,1)}, bf16[1,975456]{1,0:T(2,128)(2,1)}, u32[]{:S(2)}, u32[]{:S(2)}) collective-permute-start(bf16[1,975456]{1,0:T(2,128)(2,1)} %collective-permute-done), channel_id=1, source_target_pairs={{0,1},{1,2},{2,3},{3,0},{4,5},{5,6},{6,7},{7,4},{8,9},{9,10},{10,1... | collective-permute-start | bytes 5852744 | tf_op jit(solution)/shard_map/ppermute | solution.py:275
  (116 other events, 673.5 us)
Sparse Core Ops, SparseCore 0:
  9.6 221.6 all-gather.6
  233.4 26.1 all-gather.8
  261.2 114.8 all-gather.10
  377.5 474.3 all-gather.12
  853.3 242.0 all-gather.14
  1346.1 18.7 reduce-scatter.27
  1367.8 20.0 reduce-scatter.25
  1390.2 17.0 reduce-scatter.23
  1410.2 25.3 reduce-scatter.15
  1438.4 109.3 reduce-scatter.17
  1550.3 212.3 reduce-scatter.13
  1765.0 238.2 reduce-scatter.21
  2005.8 465.8 reduce-scatter.19
  2527.3 376.1 all-reduce.95
